TPU v7x, 32 devices: a whole 2x2x4 slice. The times are simulated.
32 devices in a mesh: groups: 2 (over y), col: 4 (over z), row: 2 (over x), side: 2 (over core).
Axes of the slice: x: 2, y: 2, z: 4, core: 2. Of those that a mesh axis runs over, the one named last changes fastest.
Arguments:
- hidden_in: bfloat16 [256, 8192], P(('groups', 'col'), 'row'), parts along dimension 0, may hold values from -40 to 40
- norm_gain: bfloat16 [8192], P('row'), may hold values from 0.099609375 to 1.8984375
- qkv_weight: bfloat16 [8192, 10240], P('row', 'col'), may hold values from -0.0625 to 0.0625
- out_weight: bfloat16 [8192, 8192], P('row', 'col'), may hold values from -0.0625 to 0.0625
- key_cache: bfloat16 [256, 64, 1024], P(('groups', 'col'), None, 'row'), parts along dimension 0, may hold values from -320 to 320
- value_cache: bfloat16 [256, 64, 1024], P(('groups', 'col'), None, 'row'), parts along dimension 0, may hold values from -4 to 4
- cache_lengths: int32 [256], P(('groups', 'col')), parts along dimension 0, may hold values from 1 to 64, 4096 in all
- slot_request: int32 [256], P('groups'), parts along dimension 0, may hold values from 0 to 127, each once
Outputs:
- layer_rows: bfloat16 [2, 256, 8192], P('side', ('groups', 'col'), 'row'), parts along dimension 1
There are 2 independent parts, one for each index of `groups`. A program takes and returns all parts, laid end to end along the dimension named above; an argument that names none is the same for every part. Nothing has to cross between parts.
Inputs may be any that keep to these rules, and one draw needn't show every extreme that they name: Slot s of cache_lengths, key_cache and value_cache belongs to request slot_request[s]; every request has exactly one slot. Positions from cache_lengths[s] on are not filled; some slot is full in every draw.
All inputs are finite; a program needn't handle non-finite values. No bound on the sum of `cache_lengths` on one device may be relied on, other than what follows from the above.
Results may differ from a plain program's by a relative error of at most 0.035.
Values may be sent and summed in bfloat16 or wider, within the bound.
A program may use at most 128 MiB of HBM per device.

v0:
```python
import jax
import jax.numpy as jnp
from jax import lax
from jax.sharding import PartitionSpec as P

D = 8192
HEADS = 64
KV_HEADS = 8
HEAD_DIM = 128
QKV = 10240


EPSILON = 1e-05
THETA = 500000.0


def swapped(value, axis, bit):
    mask = 2**bit
    pairs = [(source, source ^ mask) for source in range(lax.axis_size(axis))]
    return lax.ppermute(value, axis, pairs)


def rope_tables(lengths, head_dim):
    half_dim = head_dim // 2
    inv_freq = jnp.exp(
        -jnp.log(jnp.float32(THETA)) * jnp.arange(half_dim, dtype=jnp.float32) / half_dim
    )
    phases = lengths.astype(jnp.float32)[:, None] * inv_freq[None, :]
    return (jnp.cos(phases), jnp.sin(phases))


def rotate(vector, cos_vals, sine_vals):
    half_dim = vector.shape[-1] // 2
    front_half = vector[..., :half_dim]
    back_half = vector[..., half_dim:]
    return jnp.concatenate(
        [
            front_half * cos_vals - back_half * sine_vals,
            back_half * cos_vals + front_half * sine_vals,
        ],
        axis=-1,
    )


def attend(packed, key_block, value_block, lengths):
    slot_count = packed.shape[0]
    cache_size = key_block.shape[1]
    groups = key_block.shape[2] // HEAD_DIM
    per_group = HEADS // KV_HEADS
    grouped = packed.reshape(slot_count, groups, per_group + 2, HEAD_DIM)
    cos_vals, sine_vals = rope_tables(lengths, HEAD_DIM)
    queries = rotate(
        grouped[:, :, :per_group].astype(jnp.float32),
        cos_vals[:, None, None, :],
        sine_vals[:, None, None, :],
    ).astype(jnp.bfloat16)
    new_keys = rotate(
        grouped[:, :, per_group].astype(jnp.float32), cos_vals[:, None, :], sine_vals[:, None, :]
    ).astype(jnp.bfloat16)
    new_values = grouped[:, :, per_group + 1]
    cache_keys = key_block.reshape(slot_count, cache_size, groups, HEAD_DIM)
    cache_values = value_block.reshape(slot_count, cache_size, groups, HEAD_DIM)
    factor = HEAD_DIM ** (-0.5)
    cache_scores = (
        jnp.einsum("sghd,slgd->sghl", queries, cache_keys, preferred_element_type=jnp.float32)
        * factor
    )
    own_scores = (
        jnp.einsum("sghd,sgd->sgh", queries, new_keys, preferred_element_type=jnp.float32) * factor
    )
    in_cache = lax.broadcasted_iota(jnp.int32, (slot_count, cache_size), 1) < lengths[:, None]
    cache_scores = jnp.where(in_cache[:, None, None, :], cache_scores, -1e30)
    row_max = jnp.maximum(jnp.max(cache_scores, axis=-1), own_scores)
    cache_exp = jnp.exp(cache_scores - row_max[..., None])
    own_exp = jnp.exp(own_scores - row_max)
    denominator = jnp.sum(cache_exp, axis=-1) + own_exp
    cache_weight = (cache_exp / denominator[..., None]).astype(jnp.bfloat16)
    own_weight = (own_exp / denominator).astype(jnp.bfloat16)
    combined = jnp.einsum(
        "sghl,slgd->sghd", cache_weight, cache_values, preferred_element_type=jnp.float32
    )
    combined = (
        combined
        + own_weight.astype(jnp.float32)[..., None] * new_values.astype(jnp.float32)[:, :, None, :]
    )
    return combined.astype(jnp.bfloat16).reshape(slot_count, groups * per_group * HEAD_DIM)


def per_device(
    hidden_in,
    norm_gain,
    qkv_weight,
    out_weight,
    key_cache,
    value_cache,
    cache_lengths,
    slot_request,
):
    side_index = lax.axis_index("side")
    is_weight = side_index == 0
    col_count = lax.axis_size("col")
    row_count = lax.axis_size("row")
    group_cols = col_count // row_count
    in_half = qkv_weight.shape[1] // 2
    out_half = out_weight.shape[1] // 2
    residual = hidden_in.astype(jnp.float32)
    square_sums = lax.psum(jnp.sum(residual * residual, axis=1), "row")
    normed = (
        residual
        * lax.rsqrt(square_sums[:, None] / D + EPSILON)
        * norm_gain.astype(jnp.float32)[None, :]
    ).astype(jnp.bfloat16)
    in_weight = lax.dynamic_slice_in_dim(qkv_weight, side_index * in_half, in_half, 1)
    partial_in = jnp.dot(
        lax.all_gather(normed, "col", axis=0, tiled=True),
        in_weight,
        preferred_element_type=jnp.float32,
    )
    in_slots = jnp.take(partial_in, slot_request, axis=0)
    own_width = QKV // row_count
    summed = lax.psum(in_slots.astype(jnp.bfloat16), "row")
    spread = lax.all_to_all(summed, "col", split_axis=0, concat_axis=1, tiled=True)
    own_columns = lax.dynamic_slice_in_dim(
        spread.reshape(spread.shape[0], col_count, in_half),
        lax.axis_index("row") * group_cols,
        group_cols,
        1,
    )
    slot_half = key_cache.shape[0] // 2
    halves = lax.all_to_all(
        own_columns[:, :, None, :], "side", split_axis=0, concat_axis=2, tiled=True
    )
    arrived = halves.reshape(slot_half, own_width)
    first_slot = side_index * slot_half
    key_part = lax.dynamic_slice_in_dim(key_cache, first_slot, slot_half, 0)
    value_part = lax.dynamic_slice_in_dim(value_cache, first_slot, slot_half, 0)
    length_part = lax.dynamic_slice_in_dim(cache_lengths, first_slot, slot_half, 0)
    attended = attend(arrived, key_part, value_part, length_part)
    out_cols = lax.dynamic_slice_in_dim(out_weight, side_index * out_half, out_half, 1)
    collected = lax.all_gather(attended, ("col", "side"), axis=0, tiled=True)
    out_slots = jnp.dot(collected, out_cols, preferred_element_type=jnp.float32)
    inverse = jnp.argsort(slot_request)
    out_requests = jnp.take(out_slots, inverse, axis=0)
    spread_out = lax.all_to_all(
        out_requests.astype(jnp.bfloat16), "col", split_axis=0, concat_axis=1, tiled=True
    ).astype(out_requests.dtype)
    out_view = spread_out.reshape(spread_out.shape[0], col_count, out_half)
    summed_out = lax.psum_scatter(
        out_view.astype(jnp.bfloat16), "row", scatter_dimension=1, tiled=True
    ).astype(jnp.float32)
    req_rows = hidden_in.shape[0]
    residual_view = residual.reshape(req_rows, group_cols, 2, out_half)
    residual_half = lax.dynamic_index_in_dim(residual_view, side_index, 2, keepdims=False)
    own_hidden = (residual_half + summed_out).astype(jnp.bfloat16)
    payload = jnp.where(is_weight, attended, own_hidden.reshape(attended.shape))
    received = swapped(payload, "side", 0)
    hidden = jnp.stack([own_hidden, received.reshape(own_hidden.shape)], axis=2).reshape(
        req_rows, residual.shape[1]
    )
    attention_rows = jnp.concatenate([received, attended], axis=0)
    result = jnp.where(is_weight, hidden, attention_rows)
    return result[None]


def solution(mesh):
    placed = (
        P(("groups", "col"), "row"),
        P("row"),
        P("row", "col"),
        P("row", "col"),
        P(("groups", "col"), None, "row"),
        P(("groups", "col"), None, "row"),
        P(("groups", "col")),
        P("groups"),
    )
    return jax.shard_map(
        per_device,
        mesh=mesh,
        in_specs=placed,
        out_specs=P("side", ("groups", "col"), "row"),
        check_vma=False,
    )
```

profile of v0, /device:TPU:0, one launch (start us, length us, event | category | flops | bytes accessed | tf_op | source)
XLA Modules:
  0.0 160.2 jit_solution(10407784582039779955)
XLA Ops:
  6.5 0.7 convert_element_type.54
  7.2 1.1 multiply_reduce_fusion
  8.4 5.9 %psum.14 = f32[32]{0:T(128)S(1)} all-reduce(f32[32]{0:T(128)S(1)} %multiply_reduce_fusion), channel_id=1, replica_groups=mesh['groups'=2,'col'=4,'row'=2,'side'=2] {'row'}, use_global_device_ids=true, to_apply=%region_2.3 | all-reduce | flops 32 | bytes 256 | tf_op jit(solution)/shard_map/psum | solution.py:107
  14.2 1.8 %multiply_convert_fusion = bf16[32,4096]{1,0:T(8,128)(2,1)} fusion(f32[4096]{0:T(1024)S(1)} %convert_element_type.54, f32[32]{0:T(128)S(1)} %add_rsqrt_fusion, bf16[32,4096]{1,0:T(8,128)(2,1)} %param.8), kind=kLoop, calls=%fused_computation.18 | loop fusion | flops 524288 | bytes 540800 | tf_op jit(solution)/shard_map/convert_element_type | solution.py:112
  16.1 0.7 compare_select_fusion
  16.8 0.7 compare_and_fusion
  17.4 28.5 %all-gather.3.cloned.1.call-done = bf16[128,4096]{1,0:T(8,128)(2,1)} async-done(((bf16[32,4096]{1,0:T(8,128)(2,1)}), bf16[128,4096]{1,0:T(8,128)(2,1)}) %all-gather.3.cloned.1.call-update) | async-done | bytes 1048592 | tf_op jit(solution)/shard_map/all_gather | solution.py:115
  46.0 5.9 %fusion = bf16[128,1280]{1,0:T(8,128)(2,1)S(1)} fusion(bf16[128,4096]{1,0:T(8,128)(2,1)} %all-gather.3.cloned.1.call-done, bf16[4096,2560]{1,0:T(8,128)(2,1)} %param.10, s32[]{:T(128)S(6)} %select_n.68), kind=kOutput, calls=%fused_computation.2 | convolution fusion | flops 1342177280 | bytes 11862020 | tf_op jit(solution)/shard_map/dot_general | solution.py:114
  51.9 0.9 gather_fusion
  52.8 0.9 select_convert_fusion
  53.6 0.1 fusion.22
  53.7 1.9 %dynamic-slice_bitcast_fusion = (bf16[16,8,4,8,128]{4,3,2,1,0:T(8,128)(2,1)S(1)}, bf16[16,8,4,8,128]{4,3,2,1,0:T(8,128)(2,1)S(1)}) fusion(bf16[32,64,512]{2,1,0:T(8,128)(2,1)} %param.13, s32[]{:T(128)S(6)} %select_n.66, bf16[32,64,512]{2,1,0:T(8,128)(2,1)} %param.12), kind=kLoop, calls=%fused_computation.14 | loop fusion | bytes 4194308
  55.6 21.9 %all-reduce.2.cloned.1.call-done = bf16[4,32,1280]{2,1,0:T(8,128)(2,1)} async-done(((bf16[4,32,1280]{2,1,0:T(8,128)(2,1)}), bf16[4,32,1280]{2,1,0:T(8,128)(2,1)}) %all-reduce.2.cloned.1.call-update) | async-done | bytes 327696 | tf_op jit(solution)/shard_map/psum | solution.py:121
  77.5 4.6 %all-to-all-start = ((bf16[4,32,1280]{2,1,0:T(8,128)(2,1)}), bf16[4,32,1280]{2,1,0:T(8,128)(2,1)S(1)}, u32[]{:S(2)}, u32[]{:S(2)}) async-start(bf16[4,32,1280]{2,1,0:T(8,128)(2,1)} %all-reduce.2.cloned.1.call-done), calls=%async_computation | async-start | bytes 655360 | tf_op jit(solution)/shard_map/all_to_all | solution.py:122
  82.1 0.1 iota_compare_fusion
  82.2 0.1 multiply_cosine_fusion
  82.3 10.0 %all-to-all-done = bf16[4,32,1280]{2,1,0:T(8,128)(2,1)S(1)} async-done(((bf16[4,32,1280]{2,1,0:T(8,128)(2,1)}), bf16[4,32,1280]{2,1,0:T(8,128)(2,1)S(1)}, u32[]{:S(2)}, u32[]{:S(2)}) %all-to-all-start) | async-done | bytes 327712 | tf_op jit(solution)/shard_map/all_to_all | solution.py:122
  92.3 0.2 copy.32
  92.5 3.8 %all_to_all.41 = bf16[32,2,1,1280]{3,1,2,0:T(2,128)(2,1)S(1)} all-to-all(bf16[32,2,1,1280]{3,1,2,0:T(2,128)(2,1)S(1)} %copy.32), channel_id=1, replica_groups=mesh['groups'=2,'col'=4,'row'=2,'side'=2] {'side'}, dimensions={0} | all-to-all | bytes 327680 | tf_op jit(solution)/shard_map/all_to_all | solution.py:130
  96.4 0.1 reshape_reshape.3
  96.6 0.1 subtract_convert_fusion.1
  96.7 0.1 subtract_convert_fusion
  96.8 0.1 maximum_bitcast_fusion
  96.9 0.3 fusion.14
  97.2 0.8 fusion.23
  98.0 0.3 fusion.11
  98.4 0.5 fusion.5
  98.8 0.7 copy.64
  99.6 2.5 %sort.17 = (s32[128]{0:T(128)}, s32[128]{0:T(128)S(1)}) sort(s32[128]{0:T(128)S(1)} %copy-done.2, s32[128]{0:T(128)S(1)} %iota.16), dimensions={0}, to_apply=%region_0.0 | sort | flops 896 | bytes 2048 | tf_op jit(solution)/shard_map/jit(argsort)/sort | solution.py:142
  102.2 0.1 broadcast_in_dim.56
  102.3 17.8 %all-gather.5.cloned.1.call-done = bf16[128,4096]{1,0:T(8,128)(2,1)} async-done(((bf16[16,4096]{1,0:T(8,128)(2,1)}), bf16[128,4096]{1,0:T(8,128)(2,1)}) %all-gather.5.cloned.1.call-update) | async-done | bytes 1048592 | tf_op jit(solution)/shard_map/all_gather | solution.py:140
  120.1 5.0 %fusion.2 = bf16[128,1024]{1,0:T(8,128)(2,1)S(1)} fusion(bf16[128,4096]{1,0:T(8,128)(2,1)} %all-gather.5.cloned.1.call-done, bf16[4096,2048]{1,0:T(8,128)(2,1)} %param.11, s32[]{:T(128)S(6)} %select_n.72), kind=kOutput, calls=%fused_computation.4 | convolution fusion | flops 1073741824 | bytes 9699332 | tf_op jit(solution)/shard_map/dot_general | solution.py:141
  125.0 0.9 gather_fusion.1
  125.9 0.1 select_convert_fusion.1
  126.0 12.6 %all_to_all.42 = bf16[4,32,1024]{2,1,0:T(8,128)(2,1)} all-to-all(bf16[4,32,1024]{2,1,0:T(8,128)(2,1)S(1)} %select_convert_fusion.1), channel_id=1, replica_groups=mesh['groups'=2,'col'=4,'row'=2,'side'=2] {'col'}, dimensions={0} | all-to-all | bytes 524288 | tf_op jit(solution)/shard_map/all_to_all | solution.py:144
  138.7 0.5 reshape.201
  139.2 0.3 constant_dynamic-slice_fusion
  139.5 10.1 %reduce-scatter.2.cloned.1.call-done = bf16[32,2,1024]{2,0,1:T(8,128)(2,1)} async-done(((bf16[32,4,1024]{2,0,1:T(8,128)(2,1)}), bf16[32,2,1024]{2,0,1:T(8,128)(2,1)}) %reduce-scatter.2.cloned.1.call-update) | async-done | bytes 131088 | tf_op jit(solution)/shard_map/reduce_scatter | solution.py:148
  149.6 1.0 fusion.10
  150.6 0.1 copy.38
  150.7 0.1 reshape.205
  150.9 0.1 collective-permute-start
  150.9 0.1 concatenate.25
  151.0 1.3 collective-permute-done
  152.3 0.1 stack_reshape.3
  152.4 0.3 copy.40
  152.7 0.2 reshape.206
  152.9 0.8 maximum_select_fusion
  (31 shorter events, 0.5 us)
Async XLA Ops:
  6.5 47.1 %copy-start.1 = (s32[32]{0:T(128)S(1)}, s32[32]{0:T(128)}, u32[]{:S(2)}) copy-start(s32[32]{0:T(128)} %param.14) | copy-start | bytes 388
  6.5 39.4 %all-gather.3.cloned.1.call-start = ((), (), s32[]{:S(2)}) async-start(), calls=%async_computation.4 | async-start | bytes 1310720 | tf_op jit(solution)/shard_map/all_gather | solution.py:115
  16.0 61.5 %all-reduce.2.cloned.1.call-start = ((), (), s32[]{:S(2)}) async-start(), calls=%async_computation.5 | async-start | bytes 655360 | tf_op jit(solution)/shard_map/psum | solution.py:121
  51.8 47.8 %copy-start.2 = (s32[128]{0:T(128)S(1)}, s32[128]{0:T(128)}, u32[]{:S(2)}) copy-start(s32[128]{0:T(128)} %param.15) | copy-start | bytes 1540
  77.5 14.8 %all-to-all-start = ((bf16[4,32,1280]{2,1,0:T(8,128)(2,1)}), bf16[4,32,1280]{2,1,0:T(8,128)(2,1)S(1)}, u32[]{:S(2)}, u32[]{:S(2)}) async-start(bf16[4,32,1280]{2,1,0:T(8,128)(2,1)} %all-reduce.2.cloned.1.call-done), calls=%async_computation | async-start | bytes 655360 | tf_op jit(solution)/shard_map/all_to_all | solution.py:122
  82.1 37.9 %all-gather.5.cloned.1.call-start = ((), (), s32[]{:S(2)}) async-start(), calls=%async_computation.6 | async-start | bytes 1179648 | tf_op jit(solution)/shard_map/all_gather | solution.py:140
  96.5 42.2 %copy-start = (bf16[32,4096]{1,0:T(8,128)(2,1)S(1)}, bf16[32,4096]{1,0:T(8,128)(2,1)}, u32[]{:S(2)}) copy-start(bf16[32,4096]{1,0:T(8,128)(2,1)} %param.8) | copy-start | bytes 786436
  99.6 50.0 %reduce-scatter.2.cloned.1.call-start = ((), (), s32[]{:S(2)}) async-start(), calls=%async_computation.7 | async-start | bytes 393216 | tf_op jit(solution)/shard_map/reduce_scatter | solution.py:148
  150.9 1.4 collective-permute-start
Sparse Core Ops, SparseCore 0:
  16.2 29.7 all-gather.2
  53.8 23.7 all-reduce.1
  99.7 20.3 all-gather.4
  138.8 10.7 reduce-scatter.1
where the time goes:
time: 161 us; the launch traced here: 160 us
  waiting for transfers between devices  89.6 us (56%)
  blocking collectives  22.3 us (14%)
  between operations  13.4 us (8%)
  matrix products  12.4 us (8%)
  other arithmetic  11.3 us (7%)
  local copies, waits for them, and re-layouts  6.42 us (4%)
  starting transfers between devices  4.76 us (3%)
    all_gather x1, waiting for transfers between devices, per_device(): lax.all_gather(normed, 'col', axis=0, tiled=True)  28.5 us
    psum x1, waiting for transfers between devices, per_device(): summed = lax.psum(in_slots.astype(jnp.bfloat16), 'row')  21.9 us
    all_gather x1, waiting for transfers between devices, per_device(): collected = lax.all_gather(attended, ('col', 'side'), axis=0, tiled=True)  17.8 us
    all_to_all x1, blocking collectives, per_device(): lax.all_to_all(out_requests.astype(jnp.bfloat16), 'col', split_axis=0, co...  12.6 us
    reduce_scatter x1, waiting for transfers between devices, per_device(): lax.psum_scatter(out_view.astype(jnp.bfloat16), 'row', scatter_dimension=...  10.1 us
    all_to_all x1, waiting for transfers between devices, per_device(): lax.all_to_all(summed, 'col', split_axis=0, concat_axis=1, tiled=True)  9.99 us
    psum x1, blocking collectives, per_device(): square_sums = lax.psum(jnp.sum(residual * residual, axis=1), 'row')  5.87 us
    dot_general x1, matrix products, per_device(): jnp.dot(lax.all_gather(normed, 'col', axis=0, tiled=True), in_weight, pre...  5.86 us
  transfers between devices with their start and end apart: 6, of which 6 were waited for; matrix products, arithmetic and copies ran while one was open for 4% of the time, Pallas kernels for 0%

commit v1 on v0

--- a/solution.py
+++ b/solution.py
@@ -1,6 +1,10 @@
+import functools
+
 import jax
 import jax.numpy as jnp
 from jax import lax
+from jax.experimental import pallas as pl
+from jax.experimental.pallas import tpu as pltpu
 from jax.sharding import PartitionSpec as P
 
 D = 8192
@@ -86,7 +90,7 @@
     return combined.astype(jnp.bfloat16).reshape(slot_count, groups * per_group * HEAD_DIM)
 
 
-def per_device(
+def per_device_general(
     hidden_in,
     norm_gain,
     qkv_weight,
@@ -162,6 +166,545 @@
     return result[None]
 
 
+MESH = pl.DeviceIdType.MESH
+F32 = jnp.float32
+BF16 = jnp.bfloat16
+TILE = 256
+
+
+def fused_kernel(
+    nz,
+    nx,
+    hid_any,
+    gain_ref,
+    wq_any,
+    wo_any,
+    k_any,
+    v_any,
+    cos_ref,
+    sin_ref,
+    len_ref,
+    to_slot_ref,
+    to_req_ref,
+    out_ref,
+    wq,
+    wo,
+    kbuf,
+    vbuf,
+    hid,
+    xg,
+    xn,
+    sso,
+    ssb,
+    acc,
+    pbuf,
+    rbuf,
+    fbuf,
+    tb,
+    af,
+    ag,
+    yacc,
+    ybuf,
+    hbuf,
+    gbuf,
+    load_sem,
+    x_recv,
+    x_send,
+    x_fwd,
+    ss_recv,
+    ss_send,
+    p_recv,
+    p_send,
+    f_recv,
+    f_send,
+    a_recv,
+    a_send,
+    a_fwd,
+    y_recv,
+    y_send,
+    g_recv,
+    g_send,
+):
+    g = lax.axis_index("groups")
+    z = lax.axis_index("col")
+    x = lax.axis_index("row")
+    s = lax.axis_index("side")
+    peer = 1 - s
+    gc = nz // nx
+    per_group = HEADS // KV_HEADS
+    rows = hid_any.shape[0]
+    total = nz * rows
+    kh = hid_any.shape[1] // 2
+    in_half = wq.shape[1]
+    out_half = wo.shape[1]
+    head_cols = per_group * HEAD_DIM
+
+    def z_at(step):
+        return lax.rem(z + step, nz)
+
+    def x_at(step):
+        return lax.rem(x + step, nx)
+
+    def remote(src, dst, send, recv, zz, xx, ss):
+        return pltpu.make_async_remote_copy(
+            src_ref=src,
+            dst_ref=dst,
+            send_sem=send,
+            recv_sem=recv,
+            device_id=(g, zz, xx, ss),
+            device_id_type=MESH,
+        )
+
+    def arrived(ref, sem):
+        pltpu.make_async_copy(ref, ref, sem).wait()
+
+    own_x = [
+        pltpu.make_async_copy(
+            hid_any.at[:, pl.ds(pl.multiple_of(side * kh, 128), kh)], xg.at[side, z], x_recv.at[side, z]
+        )
+        for side in range(2)
+    ]
+    for copy in own_x:
+        copy.start()
+
+    barrier = pltpu.get_barrier_semaphore()
+    greeted = 0
+    for step in range(1, nz):
+        pl.semaphore_signal(barrier, inc=1, device_id=(g, z_at(step), x, s), device_id_type=MESH)
+        greeted += 1
+    for step in range(1, nx):
+        for side in range(2):
+            pl.semaphore_signal(
+                barrier, inc=1, device_id=(g, z, x_at(step), side), device_id_type=MESH
+            )
+            greeted += 1
+    pl.semaphore_signal(barrier, inc=1, device_id=(g, z, x, peer), device_id_type=MESH)
+    greeted += 1
+    pl.semaphore_wait(barrier, greeted)
+
+    waits = []
+    for step in range(1, nz):
+        copy = remote(
+            hid_any.at[:, pl.ds(pl.multiple_of(s * kh, 128), kh)],
+            xg.at[s, z],
+            x_send.at[step],
+            x_recv.at[s, z],
+            z_at(step),
+            x,
+            s,
+        )
+        copy.start()
+        waits.append(copy)
+
+    loads = [
+        pltpu.make_async_copy(
+            wq_any.at[pl.ds(pl.multiple_of(part * kh, 16), kh), pl.ds(pl.multiple_of(s * in_half, 128), in_half)],
+            wq.at[pl.ds(pl.multiple_of(part * kh, 16), kh), :],
+            load_sem.at[slot],
+        )
+        for slot, part in enumerate((s, peer))
+    ]
+    for j in range(gc):
+        lanes = pl.ds(pl.multiple_of((2 * j + s) * HEAD_DIM, 128), HEAD_DIM)
+        loads.append(pltpu.make_async_copy(k_any.at[:, :, lanes], kbuf.at[j], load_sem.at[2 + 2 * j]))
+        loads.append(pltpu.make_async_copy(v_any.at[:, :, lanes], vbuf.at[j], load_sem.at[3 + 2 * j]))
+    loads.append(
+        pltpu.make_async_copy(
+            wo_any.at[:, pl.ds(pl.multiple_of(s * out_half, 128), out_half)], wo, load_sem.at[2 + 2 * gc]
+        )
+    )
+    loads.append(pltpu.make_async_copy(hid_any, hid, load_sem.at[3 + 2 * gc]))
+    for copy in loads:
+        copy.start()
+
+    def prepare(side, first):
+        for step in range(nz):
+            zz = z_at(step)
+            arrived(xg.at[side, zz], x_recv.at[side, zz])
+            if first and step > 0:
+                copy = remote(
+                    xg.at[side, zz],
+                    xg.at[side, zz],
+                    x_fwd.at[step],
+                    x_recv.at[side, zz],
+                    z,
+                    x,
+                    peer,
+                )
+                copy.start()
+                waits.append(copy)
+            value = xg[side, zz].astype(F32)
+            squares = jnp.sum(value * value, axis=1, keepdims=True)
+            spread = jnp.broadcast_to(squares, (rows, 128))
+            if first:
+                sso[zz] = spread
+            else:
+                sso[zz] = sso[zz] + spread
+            xn[side, zz] = (value * gain_ref[side]).astype(BF16)
+
+    def project_in(side, first):
+        @pl.loop(0, in_half // TILE)
+        def _(n):
+            cols = pl.ds(pl.multiple_of(n * TILE, TILE), TILE)
+            part = jnp.dot(
+                xn[side].reshape(total, kh),
+                wq[pl.ds(pl.multiple_of(side * kh, 16), kh), cols],
+                preferred_element_type=F32,
+            )
+            if first:
+                acc[:, cols] = part
+            else:
+                acc[:, cols] = acc[:, cols] + part
+
+    prepare(s, True)
+    loads[0].wait()
+    project_in(s, True)
+    prepare(peer, False)
+    ss_waits = []
+    for step in range(1, nx):
+        copy = remote(sso, ssb.at[x], ss_send.at[step], ss_recv.at[x], z, x_at(step), s)
+        copy.start()
+        waits.append(copy)
+    loads[1].wait()
+    project_in(peer, False)
+    squares = sso[...]
+    for step in range(1, nx):
+        xx = x_at(step)
+        arrived(ssb.at[xx], ss_recv.at[xx])
+        squares = squares + ssb[xx]
+    scale = lax.rsqrt(squares.reshape(total, 128) / (2 * kh * nx) + EPSILON)
+    scale = jnp.concatenate([scale] * (TILE // 128), axis=1)
+    for n in range(in_half // TILE):
+        cols = slice(n * TILE, (n + 1) * TILE)
+        part = (acc[:, cols] * scale).astype(BF16)
+        moved = jnp.dot(to_slot_ref[...], part, preferred_element_type=F32).astype(BF16)
+        pbuf[:, :, cols] = moved.reshape(nz, rows, TILE)
+
+    for step in range(1, nz):
+        zz = z_at(step)
+        copy = remote(pbuf.at[zz], rbuf.at[z], p_send.at[step], p_recv.at[z], zz, x, s)
+        copy.start()
+        waits.append(copy)
+    own_p = pltpu.make_async_copy(pbuf.at[z], rbuf.at[z], p_recv.at[z])
+    own_p.start()
+
+    for step in range(1, nx):
+        xx = x_at(step)
+        for j in range(gc):
+            source = xx * gc + j
+            arrived(rbuf.at[source], p_recv.at[source])
+            copy = remote(
+                rbuf.at[source], fbuf.at[x, j], f_send.at[step, j], f_recv.at[x, j], z, xx, s
+            )
+            copy.start()
+            waits.append(copy)
+
+    factor = HEAD_DIM ** (-0.5)
+    cache = k_any.shape[1]
+    unit = 8
+    stack = unit * per_group
+    width = unit * cache
+    row_id = lax.broadcasted_iota(jnp.int32, (stack, width), 0)
+    col_id = lax.broadcasted_iota(jnp.int32, (stack, width), 1)
+    diagonal = (row_id % unit) == (col_id // cache)
+    position = col_id % cache
+
+    def tall(value):
+        return jnp.concatenate([value] * per_group, axis=0)
+
+    def turned(value, cos_vals, sin_vals):
+        return (value * cos_vals + pltpu.roll(value, HEAD_DIM // 2, 1) * sin_vals).astype(BF16)
+
+    for j in range(gc):
+        source = x * gc + j
+        arrived(rbuf.at[source], p_recv.at[source])
+        value = rbuf[source].astype(F32)
+        for step in range(1, nx):
+            xx = x_at(step)
+            arrived(fbuf.at[xx, j], f_recv.at[xx, j])
+            value = value + fbuf[xx, j].astype(F32)
+        tb[...] = value.astype(BF16).astype(F32)
+        loads[2 + 2 * j].wait()
+        loads[3 + 2 * j].wait()
+        for it in range(rows // unit):
+            block = slice(it * unit, (it + 1) * unit)
+            cos_vals, sin_vals = cos_ref[block, :], sin_ref[block, :]
+            heads = jnp.concatenate(
+                [tb[block, h * HEAD_DIM : (h + 1) * HEAD_DIM] for h in range(per_group)], axis=0
+            )
+            queries = turned(heads, tall(cos_vals), tall(sin_vals))
+            new_key = turned(
+                tb[block, head_cols : head_cols + HEAD_DIM], cos_vals, sin_vals
+            ).astype(F32)
+            new_value = tb[block, head_cols + HEAD_DIM : head_cols + 2 * HEAD_DIM]
+            keys = kbuf[j, block].reshape(width, HEAD_DIM)
+            values = vbuf[j, block].reshape(width, HEAD_DIM)
+            scores = (
+                lax.dot_general(
+                    queries, keys, (((1,), (1,)), ((), ())), preferred_element_type=F32
+                )
+                * factor
+            )
+            own = jnp.sum(queries.astype(F32) * tall(new_key), axis=1, keepdims=True) * factor
+            filled = tall(len_ref[block, :])[:, :1]
+            scores = jnp.where(diagonal & (position < filled), scores, -1e30)
+            top = jnp.maximum(jnp.max(scores, axis=1, keepdims=True), own)
+            weights = jnp.exp(scores - top)
+            own_weight = jnp.exp(own - top)
+            denominator = jnp.sum(weights, axis=1, keepdims=True) + own_weight
+            probs = (weights / denominator).astype(BF16)
+            own_prob = (own_weight / denominator).astype(BF16).astype(F32)
+            mixed = jnp.dot(probs, values, preferred_element_type=F32) + own_prob * tall(new_value)
+            for h in range(per_group):
+                af[block, h * HEAD_DIM : (h + 1) * HEAD_DIM] = mixed[h * unit : (h + 1) * unit]
+        ag[s, j, z] = af[...].astype(BF16)
+        targets = [(z_at(step), s) for step in range(1, nz)] + [(z, peer)]
+        for n, (zz, side) in enumerate(targets):
+            copy = remote(
+                ag.at[s, j, z], ag.at[s, j, z], a_send.at[j, n], a_recv.at[s, j, z], zz, x, side
+            )
+            copy.start()
+            waits.append(copy)
+
+    for j in range(gc):
+        for step in range(1, nz):
+            zz = z_at(step)
+            arrived(ag.at[s, j, zz], a_recv.at[s, j, zz])
+            copy = remote(
+                ag.at[s, j, zz],
+                ag.at[s, j, zz],
+                a_fwd.at[j, step],
+                a_recv.at[s, j, zz],
+                z,
+                x,
+                peer,
+            )
+            copy.start()
+            waits.append(copy)
+    loads[2 + 2 * gc].wait()
+
+    def project_out(side, first):
+        @pl.loop(0, out_half // TILE)
+        def _(n):
+            cols = pl.ds(pl.multiple_of(n * TILE, TILE), TILE)
+            part = None
+            for j in range(gc):
+                depth = pl.ds(pl.multiple_of((2 * j + side) * head_cols, 16), head_cols)
+                term = jnp.dot(
+                    ag[side, j].reshape(total, head_cols), wo[depth, cols], preferred_element_type=F32
+                )
+                part = term if part is None else part + term
+            if first:
+                yacc[:, cols] = part
+            else:
+                part = (yacc[:, cols] + part).astype(BF16)
+                moved = jnp.dot(to_req_ref[...], part, preferred_element_type=F32).astype(BF16)
+                ybuf[:, :, cols] = moved.reshape(nz, rows, TILE)
+
+    project_out(s, True)
+    for j in range(gc):
+        for step in range(nz):
+            zz = z_at(step)
+            arrived(ag.at[peer, j, zz], a_recv.at[peer, j, zz])
+    project_out(peer, False)
+
+    for step in range(1, nz):
+        zz = z_at(step)
+        copy = remote(ybuf.at[zz], hbuf.at[z], y_send.at[step], y_recv.at[z], zz, x, s)
+        copy.start()
+        waits.append(copy)
+    own_y = pltpu.make_async_copy(ybuf.at[z], hbuf.at[z], y_recv.at[z])
+    own_y.start()
+
+    for step in range(1, nx):
+        xx = x_at(step)
+        for j in range(gc):
+            source = xx * gc + j
+            arrived(hbuf.at[source], y_recv.at[source])
+            copy = remote(
+                hbuf.at[source],
+                gbuf.at[x, s, j],
+                g_send.at[step, j],
+                g_recv.at[x, s, j],
+                z,
+                xx,
+                0,
+            )
+            copy.start()
+            waits.append(copy)
+
+    loads[3 + 2 * gc].wait()
+    for j in range(gc):
+        source = x * gc + j
+        arrived(hbuf.at[source], y_recv.at[source])
+
+    @pl.when(s == 1)
+    def _():
+        across = []
+        for j in range(gc):
+            copy = remote(
+                hbuf.at[x * gc + j],
+                gbuf.at[x, s, j],
+                g_send.at[0, j],
+                g_recv.at[x, s, j],
+                z,
+                x,
+                0,
+            )
+            copy.start()
+            across.append(copy)
+        for j in range(gc):
+            for side in range(2):
+                lanes = slice((2 * j + side) * head_cols, (2 * j + side + 1) * head_cols)
+                out_ref[0, :, lanes] = ag[side, j, z]
+        for copy in across:
+            copy.wait_send()
+
+    @pl.when(s == 0)
+    def _():
+        for j in range(gc):
+            for side in range(2):
+                lanes = slice((2 * j + side) * out_half, (2 * j + side + 1) * out_half)
+                value = hid[:, lanes].astype(F32)
+                if side == 0:
+                    mine = hbuf[x * gc + j].astype(F32)
+                else:
+                    arrived(gbuf.at[x, 1, j], g_recv.at[x, 1, j])
+                    mine = gbuf[x, 1, j].astype(F32)
+                for step in range(1, nx):
+                    xx = x_at(step)
+                    arrived(gbuf.at[xx, side, j], g_recv.at[xx, side, j])
+                    mine = mine + gbuf[xx, side, j].astype(F32)
+                out_ref[0, :, lanes] = (value + mine).astype(BF16)
+
+    for copy in waits:
+        copy.wait_send()
+
+
+def per_device_fused(
+    hidden_in,
+    norm_gain,
+    qkv_weight,
+    out_weight,
+    key_cache,
+    value_cache,
+    cache_lengths,
+    slot_request,
+):
+    nz = lax.axis_size("col")
+    nx = lax.axis_size("row")
+    gc = nz // nx
+    rows, columns = hidden_in.shape
+    slots, cache, _ = key_cache.shape
+    kh = columns // 2
+    total = nz * rows
+    in_half = qkv_weight.shape[1] // 2
+    out_half = out_weight.shape[1] // 2
+    head_cols = HEADS // KV_HEADS * HEAD_DIM
+    cos_vals, sin_vals = rope_tables(cache_lengths, HEAD_DIM)
+    cos_full = jnp.concatenate([cos_vals, cos_vals], axis=1)
+    sin_full = jnp.concatenate([-sin_vals, sin_vals], axis=1)
+    filled = jnp.broadcast_to(cache_lengths[:, None], (slots, 128))
+    ids = jnp.arange(total, dtype=jnp.int32)
+    to_slot = (slot_request[:, None] == ids[None, :]).astype(BF16)
+    to_req = (ids[:, None] == slot_request[None, :]).astype(BF16)
+    vmem = pl.BlockSpec(memory_space=pltpu.VMEM)
+    far = pl.BlockSpec(memory_space=pl.ANY)
+    dma = pltpu.SemaphoreType.DMA
+    return pl.pallas_call(
+        functools.partial(fused_kernel, nz, nx),
+        out_shape=jax.ShapeDtypeStruct((1, rows, columns), BF16),
+        in_specs=[far, vmem, far, far, far, far, vmem, vmem, vmem, vmem, vmem],
+        out_specs=vmem,
+        scratch_shapes=[
+            pltpu.VMEM((columns, in_half), BF16),
+            pltpu.VMEM((columns, out_half), BF16),
+            pltpu.VMEM((gc, slots, cache, HEAD_DIM), BF16),
+            pltpu.VMEM((gc, slots, cache, HEAD_DIM), BF16),
+            pltpu.VMEM((rows, columns), BF16),
+            pltpu.VMEM((2, nz, rows, kh), BF16),
+            pltpu.VMEM((2, nz, rows, kh), BF16),
+            pltpu.VMEM((nz, rows, 128), F32),
+            pltpu.VMEM((nx, nz, rows, 128), F32),
+            pltpu.VMEM((total, in_half), F32),
+            pltpu.VMEM((nz, rows, in_half), BF16),
+            pltpu.VMEM((nz, rows, in_half), BF16),
+            pltpu.VMEM((nx, gc, rows, in_half), BF16),
+            pltpu.VMEM((rows, in_half), F32),
+            pltpu.VMEM((rows, head_cols), F32),
+            pltpu.VMEM((2, gc, nz, rows, head_cols), BF16),
+            pltpu.VMEM((total, out_half), F32),
+            pltpu.VMEM((nz, rows, out_half), BF16),
+            pltpu.VMEM((nz, rows, out_half), BF16),
+            pltpu.VMEM((nx, 2, gc, rows, out_half), BF16),
+            dma((4 + 2 * gc,)),
+            dma((2, nz)),
+            dma((nz,)),
+            dma((nz,)),
+            dma((nx,)),
+            dma((nx,)),
+            dma((nz,)),
+            dma((nz,)),
+            dma((nx, gc)),
+            dma((nx, gc)),
+            dma((2, gc, nz)),
+            dma((gc, nz)),
+            dma((gc, nz)),
+            dma((nz,)),
+            dma((nz,)),
+            dma((nx, 2, gc)),
+            dma((nx, gc)),
+        ],
+        compiler_params=pltpu.CompilerParams(
+            collective_id=0, has_side_effects=True, vmem_limit_bytes=60 * 1024 * 1024
+        ),
+    )(
+        hidden_in,
+        norm_gain.reshape(2, 1, kh),
+        qkv_weight,
+        out_weight,
+        key_cache,
+        value_cache,
+        cos_full,
+        sin_full,
+        filled,
+        to_slot,
+        to_req,
+    )
+
+
+def per_device(
+    hidden_in,
+    norm_gain,
+    qkv_weight,
+    out_weight,
+    key_cache,
+    value_cache,
+    cache_lengths,
+    slot_request,
+):
+    group_width = (HEADS // KV_HEADS + 2) * HEAD_DIM
+    aligned = (
+        qkv_weight.shape[1] == 2 * group_width
+        and out_weight.shape[1] % (2 * TILE) == 0
+        and lax.axis_size("col") % lax.axis_size("row") == 0
+        and hidden_in.shape[0] % 16 == 0
+        and hidden_in.shape[1] % 256 == 0
+        and key_cache.shape[0] == hidden_in.shape[0]
+    )
+    body = per_device_fused if aligned else per_device_general
+    return body(
+        hidden_in,
+        norm_gain,
+        qkv_weight,
+        out_weight,
+        key_cache,
+        value_cache,
+        cache_lengths,
+        slot_request,
+    )
+
+
 def solution(mesh):
     placed = (
         P(("groups", "col"), "row"),

time: 161 us -> 65.3 us (0.41)
  waiting for transfers between devices: 89.6 us -> 0 us
  Pallas kernels: 0 us -> 57.8 us
  blocking collectives: 22.3 us -> 0 us
  between operations: 13.4 us -> 0.02 us
  matrix products: 12.4 us -> 0 us
  other arithmetic: 11.3 us -> 2.93 us
  starting transfers between devices: 4.76 us -> 0 us
  local copies, waits for them, and re-layouts: 6.42 us -> 4.3 us
    pallas_call x0 -> x1, Pallas kernels: none -> 57.8 us  [per_device_fused(): pl.pallas_call(functools.partial(fused_kernel, nz, nx), out_shape=jax.Sha...]
    all_gather x2 -> x0, waiting for transfers between devices: 46.3 us -> none  [the longest x1 28.5 us: per_device(): lax.all_gather(normed, 'col', axis=0, tiled=True)]
    psum x1 -> x0, waiting for transfers between devices: 21.9 us -> none  [per_device(): summed = lax.psum(in_slots.astype(jnp.bfloat16), 'row')]
    all_to_all x2 -> x0, blocking collectives: 16.4 us -> none  [the longest x1 12.6 us: per_device(): lax.all_to_all(out_requests.astype(jnp.bfloat16), 'col', split_axis=0, co...]
    dot_general x5 -> x0, matrix products: 12.4 us -> none  [the longest x1 5.86 us: per_device(): jnp.dot(lax.all_gather(normed, 'col', axis=0, tiled=True), in_weight, pre...]
    reduce_scatter x1 -> x0, waiting for transfers between devices: 10.1 us -> none  [per_device(): lax.psum_scatter(out_view.astype(jnp.bfloat16), 'row', scatter_dimension=...]
    all_to_all x1 -> x0, waiting for transfers between devices: 9.99 us -> none  [per_device(): lax.all_to_all(summed, 'col', split_axis=0, concat_axis=1, tiled=True)]
    psum x1 -> x0, blocking collectives: 5.87 us -> none  [per_device(): square_sums = lax.psum(jnp.sum(residual * residual, axis=1), 'row')]
  transfers between devices with their start and end apart: 6 -> 0, of which waited for: 6 -> 0; matrix products, arithmetic and copies ran while one was open for 4% -> 0% of each run, Pallas kernels for 0% -> 0%
where the time goes in v1:
time: 65.3 us; the launch traced here: 65 us
  Pallas kernels  57.8 us (89%)
  local copies, waits for them, and re-layouts  4.3 us (7%)
  other arithmetic  2.93 us (4%)
    pallas_call x1, Pallas kernels, per_device_fused(): pl.pallas_call(functools.partial(fused_kernel, nz, nx), out_shape=jax.Sha...  57.8 us
    unnamed x1, local copies, waits for them, and re-layouts  1.67 us
    convert_element_type x1, other arithmetic, per_device_fused(): to_req = (ids[:, None] == slot_request[None, :]).astype(BF16)  1.43 us
    broadcast_in_dim x1, local copies, waits for them, and re-layouts, per_device_fused(): filled = jnp.broadcast_to(cache_lengths[:, None], (slots, 128))  1.32 us
    reshape x1, local copies, waits for them, and re-layouts, per_device_fused(): norm_gain.reshape(2, 1, kh)  1.31 us

profile of v1, /device:TPU:0, one launch (start us, length us, event | category | flops | bytes accessed | tf_op | source)
XLA Modules:
  0.0 65.0 jit_solution(1572541177206604348)
XLA Ops:
  0.0 0.7 %convert_element_type.9 = f32[32]{0:T(128)S(1)} convert(s32[32]{0:T(128)} %param.14) | non-fusion elementwise | flops 32 | bytes 256 | tf_op jit(solution)/shard_map/convert_element_type | solution.py:32
  0.7 1.3 %reshape.13.gain_ref = bf16[2,1,2048]{2,1,0:T(2,128)(2,1)} reshape(bf16[4096]{0:T(1024)(128)(2,1)} %param.9) | data formatting | bytes 16384 | tf_op jit(solution)/shard_map/reshape | solution.py:663
  2.0 1.3 %broadcast_in_dim.2.len_ref = s32[32,128]{1,0:T(8,128)} broadcast(s32[32]{0:T(128)} %param.14), dimensions={0} | broadcast | bytes 16512 | tf_op jit(solution)/shard_map/broadcast_in_dim | solution.py:607
  3.3 0.1 fusion.2
  3.4 0.7 %pad_maximum_fusion = (f32[32,128]{1,0:T(8,128)}, f32[32,128]{1,0:T(8,128)}) fusion(f32[32,64]{1,0:T(8,128)S(1)} %get-tuple-element.7, f32[32,64]{1,0:T(8,128)S(1)} %get-tuple-element.6, f32[32,64]{1,0:T(8,128)S(1)} %get-tuple-element.5), kind=kLoop, calls=%fused_computation.6 | loop fusion | flops 8192 | bytes 57344 | tf_op jit(solution)/shard_map/concatenate | solution.py:605
  4.1 1.4 %fusion.1 = (bf16[128,128]{1,0:T(8,128)(2,1)}, bf16[128,128]{1,0:T(8,128)(2,1)}) fusion(s32[128]{0:T(128)} %param.15), kind=kLoop, calls=%fused_computation.3 | loop fusion | flops 65536 | bytes 66048 | tf_op jit(solution)/shard_map/convert_element_type | solution.py:610
  5.6 57.8 %shard_map.82 = bf16[1,32,4096]{2,1,0:T(8,128)(2,1)} custom-call(bf16[32,4096]{1,0:T(8,128)(2,1)} %hid_any.1, bf16[2,1,2048]{2,1,0:T(2,128)(2,1)} %reshape.13.gain_ref, bf16[4096,2560]{1,0:T(8,128)(2,1)} %wq_any.1, bf16[4096,2048]{1,0:T(8,128)(2,1)} %wo_any.1, bf16[32,64,512]{2,1,0:T(8,128)(2,1)} %k_any.1, bf16[32,64,512]{2,1,0:T(8,128)(2,1)} %v_any.1, ...), custom_call_target="tpu_custom_call" | custom-call | tf_op jit(solution)/shard_map/pallas_call | solution.py:614
  63.4 1.7 %copy.11 = bf16[1,32,4096]{2,1,0:T(8,128)(2,1)} copy(bf16[1,32,4096]{2,1,0:T(8,128)(2,1)} %shard_map.82) | data formatting | bytes 524288
  (1 shorter events, 0.0 us)

commit v2 on v1

--- a/solution.py
+++ b/solution.py
@@ -176,17 +176,14 @@
     nz,
     nx,
     hid_any,
-    gain_ref,
+    gain_any,
     wq_any,
     wo_any,
     k_any,
     v_any,
-    cos_ref,
-    sin_ref,
-    len_ref,
-    to_slot_ref,
-    to_req_ref,
-    out_ref,
+    len_any,
+    req_any,
+    out_any,
     wq,
     wo,
     kbuf,
@@ -207,6 +204,17 @@
     ybuf,
     hbuf,
     gbuf,
+    gain_buf,
+    len_buf,
+    req_buf,
+    cos_ref,
+    sin_ref,
+    len_ref,
+    to_slot_ref,
+    to_req_ref,
+    scale_buf,
+    out_ref,
+    small_sem,
     load_sem,
     x_recv,
     x_send,
@@ -264,8 +272,17 @@
         )
         for side in range(2)
     ]
-    for copy in own_x:
+    small = [
+        pltpu.make_async_copy(far, near, small_sem.at[slot])
+        for slot, (far, near) in enumerate(
+            ((gain_any, gain_buf), (len_any, len_buf), (req_any, req_buf))
+        )
+    ]
+    for copy in own_x + small:
         copy.start()
+
+    hid_load = pltpu.make_async_copy(hid_any, hid, load_sem.at[3 + 2 * gc])
+    hid_load.start()
 
     barrier = pltpu.get_barrier_semaphore()
     greeted = 0
@@ -280,12 +297,13 @@
             greeted += 1
     pl.semaphore_signal(barrier, inc=1, device_id=(g, z, x, peer), device_id_type=MESH)
     greeted += 1
+    hid_load.wait()
     pl.semaphore_wait(barrier, greeted)
 
     waits = []
     for step in range(1, nz):
         copy = remote(
-            hid_any.at[:, pl.ds(pl.multiple_of(s * kh, 128), kh)],
+            hid.at[:, pl.ds(pl.multiple_of(s * kh, 128), kh)],
             xg.at[s, z],
             x_send.at[step],
             x_recv.at[s, z],
@@ -313,11 +331,34 @@
             wo_any.at[:, pl.ds(pl.multiple_of(s * out_half, 128), out_half)], wo, load_sem.at[2 + 2 * gc]
         )
     )
-    loads.append(pltpu.make_async_copy(hid_any, hid, load_sem.at[3 + 2 * gc]))
     for copy in loads:
         copy.start()
 
+    for copy in small:
+        copy.wait()
+    wide = (total, total)
+    owner = jnp.broadcast_to(req_buf[...].reshape(1, total), wide)
+    to_req = (owner == lax.broadcasted_iota(jnp.int32, wide, 0)).astype(F32)
+    to_req_ref[...] = to_req.astype(BF16)
+    to_slot_ref[...] = to_req.T.astype(BF16)
+    slots = k_any.shape[0]
+    square = (slots, slots)
+    across = jnp.broadcast_to(len_buf[...].reshape(1, slots), square).astype(F32)
+    on_diagonal = lax.broadcasted_iota(jnp.int32, square, 0) == lax.broadcasted_iota(
+        jnp.int32, square, 1
+    )
+    lengths = jnp.sum(jnp.where(on_diagonal, across, 0.0), axis=1, keepdims=True)
+    lengths = jnp.broadcast_to(lengths, (slots, HEAD_DIM))
+    len_ref[...] = lengths
+    half_dim = HEAD_DIM // 2
+    lane = lax.broadcasted_iota(jnp.int32, (slots, HEAD_DIM), 1)
+    exponent = lax.rem(lane, half_dim).astype(F32)
+    phases = lengths * jnp.exp(-jnp.log(jnp.full((1, 1), THETA, F32)) * exponent / half_dim)
+    cos_ref[...] = jnp.cos(phases)
+    sin_ref[...] = jnp.where(lane < half_dim, -1.0, 1.0) * jnp.sin(phases)
+
     def prepare(side, first):
+        gain = gain_buf[pl.ds(pl.multiple_of(side * kh, 128), kh)].astype(F32).reshape(1, kh)
         for step in range(nz):
             zz = z_at(step)
             arrived(xg.at[side, zz], x_recv.at[side, zz])
@@ -340,64 +381,73 @@
                 sso[zz] = spread
             else:
                 sso[zz] = sso[zz] + spread
-            xn[side, zz] = (value * gain_ref[side]).astype(BF16)
-
-    def project_in(side, first):
+            xn[side, zz] = (value * gain).astype(BF16)
+
+    def project_in(side):
         @pl.loop(0, in_half // TILE)
         def _(n):
             cols = pl.ds(pl.multiple_of(n * TILE, TILE), TILE)
-            part = jnp.dot(
+            acc[:, cols] = jnp.dot(
                 xn[side].reshape(total, kh),
                 wq[pl.ds(pl.multiple_of(side * kh, 16), kh), cols],
                 preferred_element_type=F32,
             )
-            if first:
-                acc[:, cols] = part
-            else:
-                acc[:, cols] = acc[:, cols] + part
 
     prepare(s, True)
     loads[0].wait()
-    project_in(s, True)
+    project_in(s)
     prepare(peer, False)
-    ss_waits = []
     for step in range(1, nx):
         copy = remote(sso, ssb.at[x], ss_send.at[step], ss_recv.at[x], z, x_at(step), s)
         copy.start()
         waits.append(copy)
     loads[1].wait()
-    project_in(peer, False)
+    in_chunks = in_half // TILE
+    for n in range(in_chunks):
+        cols = slice(n * TILE, (n + 1) * TILE)
+        part = acc[:, cols] + jnp.dot(
+            xn[peer].reshape(total, kh),
+            wq[pl.ds(pl.multiple_of(peer * kh, 16), kh), cols],
+            preferred_element_type=F32,
+        )
+        moved = jnp.dot(to_slot_ref[...], part.astype(BF16), preferred_element_type=F32)
+        pbuf[n] = moved.astype(BF16).reshape(nz, rows, TILE)
+        for step in range(1, nz):
+            zz = z_at(step)
+            copy = remote(
+                pbuf.at[n, zz], rbuf.at[n, z], p_send.at[step, n], p_recv.at[z, n], zz, x, s
+            )
+            copy.start()
+            waits.append(copy)
+        pltpu.make_async_copy(pbuf.at[n, z], rbuf.at[n, z], p_recv.at[z, n]).start()
+
     squares = sso[...]
     for step in range(1, nx):
         xx = x_at(step)
         arrived(ssb.at[xx], ss_recv.at[xx])
         squares = squares + ssb[xx]
-    scale = lax.rsqrt(squares.reshape(total, 128) / (2 * kh * nx) + EPSILON)
-    scale = jnp.concatenate([scale] * (TILE // 128), axis=1)
-    for n in range(in_half // TILE):
-        cols = slice(n * TILE, (n + 1) * TILE)
-        part = (acc[:, cols] * scale).astype(BF16)
-        moved = jnp.dot(to_slot_ref[...], part, preferred_element_type=F32).astype(BF16)
-        pbuf[:, :, cols] = moved.reshape(nz, rows, TILE)
-
-    for step in range(1, nz):
-        zz = z_at(step)
-        copy = remote(pbuf.at[zz], rbuf.at[z], p_send.at[step], p_recv.at[z], zz, x, s)
-        copy.start()
-        waits.append(copy)
-    own_p = pltpu.make_async_copy(pbuf.at[z], rbuf.at[z], p_recv.at[z])
-    own_p.start()
-
-    for step in range(1, nx):
-        xx = x_at(step)
+    flat = jnp.broadcast_to(squares.reshape(total, 128).T[:1, :], (total, total))
+    by_slot = jnp.sum(to_slot_ref[...].astype(F32) * flat, axis=1, keepdims=True)
+    scale = lax.rsqrt(by_slot / (2 * kh * nx) + EPSILON)
+    scale_buf[...] = jnp.broadcast_to(scale, (total, 128)).reshape(nz, rows, 128)
+
+    for n in range(in_chunks):
         for j in range(gc):
-            source = xx * gc + j
-            arrived(rbuf.at[source], p_recv.at[source])
-            copy = remote(
-                rbuf.at[source], fbuf.at[x, j], f_send.at[step, j], f_recv.at[x, j], z, xx, s
-            )
-            copy.start()
-            waits.append(copy)
+            for step in range(1, nx):
+                xx = x_at(step)
+                source = xx * gc + j
+                arrived(rbuf.at[n, source], p_recv.at[source, n])
+                copy = remote(
+                    rbuf.at[n, source],
+                    fbuf.at[x, j, n],
+                    f_send.at[step, j, n],
+                    f_recv.at[x, j, n],
+                    z,
+                    xx,
+                    s,
+                )
+                copy.start()
+                waits.append(copy)
 
     factor = HEAD_DIM ** (-0.5)
     cache = k_any.shape[1]
@@ -407,7 +457,7 @@
     row_id = lax.broadcasted_iota(jnp.int32, (stack, width), 0)
     col_id = lax.broadcasted_iota(jnp.int32, (stack, width), 1)
     diagonal = (row_id % unit) == (col_id // cache)
-    position = col_id % cache
+    position = (col_id % cache).astype(F32)
 
     def tall(value):
         return jnp.concatenate([value] * per_group, axis=0)
@@ -417,13 +467,15 @@
 
     for j in range(gc):
         source = x * gc + j
-        arrived(rbuf.at[source], p_recv.at[source])
-        value = rbuf[source].astype(F32)
-        for step in range(1, nx):
-            xx = x_at(step)
-            arrived(fbuf.at[xx, j], f_recv.at[xx, j])
-            value = value + fbuf[xx, j].astype(F32)
-        tb[...] = value.astype(BF16).astype(F32)
+        own_scale = scale_buf[z][:, :1]
+        for n in range(in_chunks):
+            arrived(rbuf.at[n, source], p_recv.at[source, n])
+            value = rbuf[n, source].astype(F32)
+            for step in range(1, nx):
+                xx = x_at(step)
+                arrived(fbuf.at[xx, j, n], f_recv.at[xx, j, n])
+                value = value + fbuf[xx, j, n].astype(F32)
+            tb[:, n * TILE : (n + 1) * TILE] = (value * own_scale).astype(BF16).astype(F32)
         loads[2 + 2 * j].wait()
         loads[3 + 2 * j].wait()
         for it in range(rows // unit):
@@ -483,76 +535,76 @@
             waits.append(copy)
     loads[2 + 2 * gc].wait()
 
-    def project_out(side, first):
-        @pl.loop(0, out_half // TILE)
-        def _(n):
-            cols = pl.ds(pl.multiple_of(n * TILE, TILE), TILE)
-            part = None
-            for j in range(gc):
-                depth = pl.ds(pl.multiple_of((2 * j + side) * head_cols, 16), head_cols)
-                term = jnp.dot(
-                    ag[side, j].reshape(total, head_cols), wo[depth, cols], preferred_element_type=F32
-                )
-                part = term if part is None else part + term
-            if first:
-                yacc[:, cols] = part
-            else:
-                part = (yacc[:, cols] + part).astype(BF16)
-                moved = jnp.dot(to_req_ref[...], part, preferred_element_type=F32).astype(BF16)
-                ybuf[:, :, cols] = moved.reshape(nz, rows, TILE)
-
-    project_out(s, True)
+    def out_part(side, cols):
+        part = None
+        for j in range(gc):
+            depth = pl.ds(pl.multiple_of((2 * j + side) * head_cols, 16), head_cols)
+            term = jnp.dot(
+                ag[side, j].reshape(total, head_cols), wo[depth, cols], preferred_element_type=F32
+            )
+            part = term if part is None else part + term
+        return part
+
+    @pl.loop(0, out_half // TILE)
+    def _(n):
+        cols = pl.ds(pl.multiple_of(n * TILE, TILE), TILE)
+        yacc[:, cols] = out_part(s, cols)
+
     for j in range(gc):
         for step in range(nz):
             zz = z_at(step)
             arrived(ag.at[peer, j, zz], a_recv.at[peer, j, zz])
-    project_out(peer, False)
-
-    for step in range(1, nz):
-        zz = z_at(step)
-        copy = remote(ybuf.at[zz], hbuf.at[z], y_send.at[step], y_recv.at[z], zz, x, s)
-        copy.start()
-        waits.append(copy)
-    own_y = pltpu.make_async_copy(ybuf.at[z], hbuf.at[z], y_recv.at[z])
-    own_y.start()
-
-    for step in range(1, nx):
-        xx = x_at(step)
-        for j in range(gc):
-            source = xx * gc + j
-            arrived(hbuf.at[source], y_recv.at[source])
+    out_chunks = out_half // TILE
+    for n in range(out_chunks):
+        cols = slice(n * TILE, (n + 1) * TILE)
+        part = (yacc[:, cols] + out_part(peer, cols)).astype(BF16)
+        moved = jnp.dot(to_req_ref[...], part, preferred_element_type=F32)
+        ybuf[n] = moved.astype(BF16).reshape(nz, rows, TILE)
+        for step in range(1, nz):
+            zz = z_at(step)
             copy = remote(
-                hbuf.at[source],
-                gbuf.at[x, s, j],
-                g_send.at[step, j],
-                g_recv.at[x, s, j],
-                z,
-                xx,
-                0,
+                ybuf.at[n, zz], hbuf.at[n, z], y_send.at[step, n], y_recv.at[z, n], zz, x, s
             )
             copy.start()
             waits.append(copy)
-
-    loads[3 + 2 * gc].wait()
-    for j in range(gc):
-        source = x * gc + j
-        arrived(hbuf.at[source], y_recv.at[source])
+        pltpu.make_async_copy(ybuf.at[n, z], hbuf.at[n, z], y_recv.at[z, n]).start()
+
+    for n in range(out_chunks):
+        for j in range(gc):
+            for step in range(1, nx):
+                xx = x_at(step)
+                source = xx * gc + j
+                arrived(hbuf.at[n, source], y_recv.at[source, n])
+                copy = remote(
+                    hbuf.at[n, source],
+                    gbuf.at[x, s, j, n],
+                    g_send.at[step, j, n],
+                    g_recv.at[x, s, j, n],
+                    z,
+                    xx,
+                    0,
+                )
+                copy.start()
+                waits.append(copy)
 
     @pl.when(s == 1)
     def _():
         across = []
-        for j in range(gc):
-            copy = remote(
-                hbuf.at[x * gc + j],
-                gbuf.at[x, s, j],
-                g_send.at[0, j],
-                g_recv.at[x, s, j],
-                z,
-                x,
-                0,
-            )
-            copy.start()
-            across.append(copy)
+        for n in range(out_chunks):
+            for j in range(gc):
+                source = x * gc + j
+                arrived(hbuf.at[n, source], y_recv.at[source, n])
+                copy = remote(
+                    hbuf.at[n, source],
+                    gbuf.at[x, s, j, n],
+                    g_send.at[0, j, n],
+                    g_recv.at[x, s, j, n],
+                    z,
+                    x,
+                    0,
+                )
+                copy.start()
+                across.append(copy)
         for j in range(gc):
             for side in range(2):
                 lanes = slice((2 * j + side) * head_cols, (2 * j + side + 1) * head_cols)
@@ -562,23 +614,30 @@
 
     @pl.when(s == 0)
     def _():
-        for j in range(gc):
-            for side in range(2):
-                lanes = slice((2 * j + side) * out_half, (2 * j + side + 1) * out_half)
-                value = hid[:, lanes].astype(F32)
-                if side == 0:
-                    mine = hbuf[x * gc + j].astype(F32)
-                else:
-                    arrived(gbuf.at[x, 1, j], g_recv.at[x, 1, j])
-                    mine = gbuf[x, 1, j].astype(F32)
-                for step in range(1, nx):
-                    xx = x_at(step)
-                    arrived(gbuf.at[xx, side, j], g_recv.at[xx, side, j])
-                    mine = mine + gbuf[xx, side, j].astype(F32)
-                out_ref[0, :, lanes] = (value + mine).astype(BF16)
-
+        for n in range(out_chunks):
+            for j in range(gc):
+                source = x * gc + j
+                for side in range(2):
+                    begin = (2 * j + side) * out_half + n * TILE
+                    lanes = slice(begin, begin + TILE)
+                    value = hid[:, lanes].astype(F32)
+                    if side == 0:
+                        arrived(hbuf.at[n, source], y_recv.at[source, n])
+                        mine = hbuf[n, source].astype(F32)
+                    else:
+                        arrived(gbuf.at[x, 1, j, n], g_recv.at[x, 1, j, n])
+                        mine = gbuf[x, 1, j, n].astype(F32)
+                    for step in range(1, nx):
+                        xx = x_at(step)
+                        arrived(gbuf.at[xx, side, j, n], g_recv.at[xx, side, j, n])
+                        mine = mine + gbuf[xx, side, j, n].astype(F32)
+                    out_ref[0, :, lanes] = (value + mine).astype(BF16)
+
+    written = pltpu.make_async_copy(out_ref, out_any, small_sem.at[3])
+    written.start()
     for copy in waits:
         copy.wait_send()
+    written.wait()
 
 
 def per_device_fused(
@@ -601,21 +660,14 @@
     in_half = qkv_weight.shape[1] // 2
     out_half = out_weight.shape[1] // 2
     head_cols = HEADS // KV_HEADS * HEAD_DIM
-    cos_vals, sin_vals = rope_tables(cache_lengths, HEAD_DIM)
-    cos_full = jnp.concatenate([cos_vals, cos_vals], axis=1)
-    sin_full = jnp.concatenate([-sin_vals, sin_vals], axis=1)
-    filled = jnp.broadcast_to(cache_lengths[:, None], (slots, 128))
-    ids = jnp.arange(total, dtype=jnp.int32)
-    to_slot = (slot_request[:, None] == ids[None, :]).astype(BF16)
-    to_req = (ids[:, None] == slot_request[None, :]).astype(BF16)
-    vmem = pl.BlockSpec(memory_space=pltpu.VMEM)
+    nc, ny = in_half // TILE, out_half // TILE
     far = pl.BlockSpec(memory_space=pl.ANY)
     dma = pltpu.SemaphoreType.DMA
     return pl.pallas_call(
         functools.partial(fused_kernel, nz, nx),
         out_shape=jax.ShapeDtypeStruct((1, rows, columns), BF16),
-        in_specs=[far, vmem, far, far, far, far, vmem, vmem, vmem, vmem, vmem],
-        out_specs=vmem,
+        in_specs=[pl.BlockSpec(memory_space=pltpu.HBM)] * 8,
+        out_specs=far,
         scratch_shapes=[
             pltpu.VMEM((columns, in_half), BF16),
             pltpu.VMEM((columns, out_half), BF16),
@@ -627,49 +679,57 @@
             pltpu.VMEM((nz, rows, 128), F32),
             pltpu.VMEM((nx, nz, rows, 128), F32),
             pltpu.VMEM((total, in_half), F32),
-            pltpu.VMEM((nz, rows, in_half), BF16),
-            pltpu.VMEM((nz, rows, in_half), BF16),
-            pltpu.VMEM((nx, gc, rows, in_half), BF16),
+            pltpu.VMEM((nc, nz, rows, TILE), BF16),
+            pltpu.VMEM((nc, nz, rows, TILE), BF16),
+            pltpu.VMEM((nx, gc, nc, rows, TILE), BF16),
             pltpu.VMEM((rows, in_half), F32),
             pltpu.VMEM((rows, head_cols), F32),
             pltpu.VMEM((2, gc, nz, rows, head_cols), BF16),
             pltpu.VMEM((total, out_half), F32),
-            pltpu.VMEM((nz, rows, out_half), BF16),
-            pltpu.VMEM((nz, rows, out_half), BF16),
-            pltpu.VMEM((nx, 2, gc, rows, out_half), BF16),
+            pltpu.VMEM((ny, nz, rows, TILE), BF16),
+            pltpu.VMEM((ny, nz, rows, TILE), BF16),
+            pltpu.VMEM((nx, 2, gc, ny, rows, TILE), BF16),
+            pltpu.VMEM((columns,), BF16),
+            pltpu.VMEM((slots,), jnp.int32),
+            pltpu.VMEM((total,), jnp.int32),
+            pltpu.VMEM((slots, HEAD_DIM), F32),
+            pltpu.VMEM((slots, HEAD_DIM), F32),
+            pltpu.VMEM((slots, HEAD_DIM), F32),
+            pltpu.VMEM((total, total), BF16),
+            pltpu.VMEM((total, total), BF16),
+            pltpu.VMEM((nz, rows, 128), F32),
+            pltpu.VMEM((1, rows, columns), BF16),
+            dma((4,)),
             dma((4 + 2 * gc,)),
             dma((2, nz)),
             dma((nz,)),
             dma((nz,)),
             dma((nx,)),
             dma((nx,)),
-            dma((nz,)),
-            dma((nz,)),
-            dma((nx, gc)),
-            dma((nx, gc)),
+            dma((nz, nc)),
+            dma((nz, nc)),
+            dma((nx, gc, nc)),
+            dma((nx, gc, nc)),
             dma((2, gc, nz)),
             dma((gc, nz)),
             dma((gc, nz)),
-            dma((nz,)),
-            dma((nz,)),
-            dma((nx, 2, gc)),
-            dma((nx, gc)),
+            dma((nz, ny)),
+            dma((nz, ny)),
+            dma((nx, 2, gc, ny)),
+            dma((nx, gc, ny)),
         ],
         compiler_params=pltpu.CompilerParams(
             collective_id=0, has_side_effects=True, vmem_limit_bytes=60 * 1024 * 1024
         ),
     )(
         hidden_in,
-        norm_gain.reshape(2, 1, kh),
+        norm_gain,
         qkv_weight,
         out_weight,
         key_cache,
         value_cache,
-        cos_full,
-        sin_full,
-        filled,
-        to_slot,
-        to_req,
+        cache_lengths,
+        slot_request,
     )
 
 

time: 65.3 us -> 56.9 us (0.87)
  other arithmetic: 2.93 us -> 0 us
  Pallas kernels: 57.8 us -> 55 us
  local copies, waits for them, and re-layouts: 4.3 us -> 1.67 us
    pallas_call x1, Pallas kernels: 57.8 us -> 55 us  [per_device_fused(): pl.pallas_call(functools.partial(fused_kernel, nz, nx), out_shape=jax.Sha...]
    convert_element_type x2 -> x0, other arithmetic: 2.09 us -> none  [the longest x1 1.43 us: per_device_fused(): to_req = (ids[:, None] == slot_request[None, :]).astype(BF16)]
    broadcast_in_dim x1 -> x0, local copies, waits for them, and re-layouts: 1.32 us -> none  [per_device_fused(): filled = jnp.broadcast_to(cache_lengths[:, None], (slots, 128))]
    reshape x1 -> x0, local copies, waits for them, and re-layouts: 1.31 us -> none  [per_device_fused(): norm_gain.reshape(2, 1, kh)]
    concatenate x1 -> x0, other arithmetic: 0.69 us -> none  [per_device_fused(): cos_full = jnp.concatenate([cos_vals, cos_vals], axis=1)]
where the time goes in v2:
time: 56.9 us; the launch traced here: 56.7 us
  Pallas kernels  55 us (97%)
  local copies, waits for them, and re-layouts  1.67 us (3%)
    pallas_call x1, Pallas kernels, per_device_fused(): pl.pallas_call(functools.partial(fused_kernel, nz, nx), out_shape=jax.Sha...  55 us
    unnamed x1, local copies, waits for them, and re-layouts  1.67 us

profile of v2, /device:TPU:0, one launch (start us, length us, event | category | flops | bytes accessed | tf_op | source)
XLA Modules:
  0.0 56.7 jit_solution(13535410668778165298)
XLA Ops:
  0.0 55.0 %shard_map.82 = bf16[1,32,4096]{2,1,0:T(8,128)(2,1)} custom-call(bf16[32,4096]{1,0:T(8,128)(2,1)} %hid_any.1, bf16[4096]{0:T(1024)(128)(2,1)} %gain_any.1, bf16[4096,2560]{1,0:T(8,128)(2,1)} %wq_any.1, bf16[4096,2048]{1,0:T(8,128)(2,1)} %wo_any.1, bf16[32,64,512]{2,1,0:T(8,128)(2,1)} %k_any.1, bf16[32,64,512]{2,1,0:T(8,128)(2,1)} %v_any.1, s32[32]{0:T(128)} %len_any.1, ...), custom_call_target="tpu_custom_call" | custom-call | tf_op jit(solution)/shard_map/pallas_call | solution.py:666
  55.0 1.7 %copy.10 = bf16[1,32,4096]{2,1,0:T(8,128)(2,1)} copy(bf16[1,32,4096]{2,1,0:T(8,128)(2,1)} %shard_map.82) | data formatting | bytes 524288
